TPU v7x, 32 devices: a whole 2x2x4 slice. The times are simulated.
32 devices in a mesh: wide: 16 (over z, y, x), clus: 2 (over core).
Axes of the slice: x: 2, y: 2, z: 4, core: 2. Of those that a mesh axis runs over, the one named last changes fastest.
Arguments:
- duals: bfloat16 [96, 64, 3840], P(None, ('wide', 'clus')), may hold values from -6 to 6
- kernel: bfloat16 [64, 6, 3840], P(('wide', 'clus')), may hold values from -0.29882812 to 0.29882812
- sub_counts: int32 [32], P(('wide', 'clus')), may hold values from 1 to 2, as said below
- dual_sizes: int32 [64], P(('wide', 'clus')), may hold values from 1920 to 3840, as said below
- cluster_factor: float32 [16, 24, 24], P('wide'), as said below
- coarse_map: int32 [16, 24], P('wide'), may hold values from 0 to 383, as said below
- coarse_inverse: float32 [384, 384], P(None, 'clus'), as said below
Outputs:
- projected: bfloat16 [96, 64, 3840], P(None, ('wide', 'clus'))
Inputs may be any that keep to these rules, and one draw needn't show every extreme that they name: `sub_counts`: each device holds 1 to 2 subdomains; some device holds 2. `dual_sizes`: some slot has the full 3840. `coarse_map`: the rows of cluster w map into the 48 global rows that begin at w * 24, counted modulo 384. `cluster_factor`: lower triangular with diagonal entries between 1 and 2. `coarse_inverse`: diagonal entries between 1 and 2.
All inputs are finite; a program needn't handle non-finite values.
Results may differ from a plain program's by a relative error of at most 0.0018.
Values sent between devices are 32-bit elements; how exact they have to be, the bound alone decides.
No kernel may reach another device: no remote copies, remote signals or barrier semaphores. Data moves between devices by JAX's collectives and lax.ppermute only.
A program may use at most 64 MiB of HBM per device.

v0:
```python
import jax
import jax.numpy as jnp
from jax import lax
from jax.sharding import PartitionSpec as P


def per_device(duals, kernel, sub_counts, dual_sizes, cluster_factor, coarse_map, coarse_inverse):
    rhs_count, sub_count, dual_width = duals.shape
    mode_count = kernel.shape[1]
    hi = lax.Precision.HIGHEST
    position = lax.broadcasted_iota(jnp.int32, (sub_count, dual_width), 1)
    slot_index = lax.broadcasted_iota(jnp.int32, (sub_count, dual_width), 0)
    active = (position < dual_sizes[:, None]) & (slot_index < sub_counts[0])
    masked = jnp.where(active[:, None, :], kernel, jnp.zeros_like(kernel))
    local = jnp.einsum("rsi,ski->rsk", duals, masked, preferred_element_type=jnp.float32)
    local = local.reshape(rhs_count, sub_count * mode_count)
    cluster_vec = lax.all_gather(local, "clus", axis=1, tiled=True)
    lower = cluster_factor[0]
    rows_map = coarse_map[0]
    cluster_rows = rows_map.shape[0]
    global_rows = coarse_inverse.shape[0]
    forward = lax.linalg.triangular_solve(lower, cluster_vec.T, left_side=True, lower=True).T
    one_hot = (
        rows_map[:, None] == lax.broadcasted_iota(jnp.int32, (cluster_rows, global_rows), 1)
    ).astype(jnp.float32)
    part_sum = jnp.dot(forward, one_hot, precision=hi)
    gsum = lax.psum(part_sum, "wide")
    beta_part = jnp.dot(gsum, coarse_inverse, precision=hi)
    beta = lax.all_gather(beta_part, "clus", axis=1, tiled=True)
    back = jnp.dot(beta, one_hot.T, precision=hi)
    corr = lax.linalg.triangular_solve(
        lower, (forward - back).T, left_side=True, lower=True, transpose_a=True
    )
    own_rows = lax.dynamic_slice_in_dim(
        corr, lax.axis_index("clus") * sub_count * mode_count, sub_count * mode_count, 0
    )
    own_corr = own_rows.T.reshape(rhs_count, sub_count, mode_count).astype(jnp.bfloat16)
    delta = jnp.einsum("rsk,ski->rsi", own_corr, masked, preferred_element_type=jnp.float32)
    return (duals.astype(jnp.float32) - delta).astype(jnp.bfloat16)


def solution(mesh):
    in_specs = (
        P(None, ("wide", "clus"), None),
        P(("wide", "clus"), None, None),
        P(("wide", "clus")),
        P(("wide", "clus")),
        P("wide", None, None),
        P("wide", None),
        P(None, "clus"),
    )
    out_specs = P(None, ("wide", "clus"), None)
    return jax.shard_map(
        per_device, mesh=mesh, in_specs=in_specs, out_specs=out_specs, check_vma=False
    )
```

profile of v0, /device:TPU:0, one launch (start us, length us, event | category | flops | bytes accessed | tf_op | source)
XLA Modules:
  0.0 140.0 jit_solution(6165059862386261918)
XLA Ops:
  6.5 0.0 copy-start
  6.5 0.0 copy-start.2
  6.5 0.0 all-reduce.2.cloned.1.call-start
  7.3 0.7 fusion.16
  8.0 1.8 %custom-call.5 = f32[1,24,24]{1,2,0:T(8,128)S(1)} custom-call(f32[1,24,24]{2,1,0:T(8,128)S(1)} %fusion.16), custom_call_target="InvertDiagBlocksLowerTriangular" | custom-call | tf_op jit(solution)/shard_map/triangular_solve | solution.py:31
  9.8 0.8 compare_and_fusion
  10.6 1.0 broadcast_select_fusion
  11.6 0.0 copy-start.1
  11.6 2.0 %fusion.4 = f32[96,2,6]{0,2,1:T(8,128)S(1)} fusion(bf16[96,2,3840]{2,1,0:T(2,128)(2,1)} %param.7, bf16[2,6,3840]{2,0,1:T(2,128)(2,1)S(1)} %broadcast_select_fusion), kind=kOutput, calls=%fused_computation.6 | convolution fusion | flops 8847360 | bytes 1571328 | tf_op jit(solution)/shard_map/rsi,ski->rsk/dot_general | solution.py:15
  13.5 2.0 %all-gather = f32[2,12,96]{2,1,0:T(8,128)S(1)} all-gather(f32[1,12,96]{2,1,0:T(8,128)S(1)} %bitcast.34), channel_id=1, replica_groups=mesh['wide'=16,'clus'=2] {'clus'}, dimensions={0}, use_global_device_ids=true | all-gather | bytes 13824 | tf_op jit(solution)/shard_map/all_gather | solution.py:17
  15.5 0.2 fusion.14
  15.7 0.0 copy-done.2
  15.7 0.9 fusion.9
  16.7 0.0 all-reduce.2.cloned.1.call-update
  16.7 109.5 %all-reduce.2.cloned.1.call-done = f32[96,384]{1,0:T(8,128)} async-done(((f32[96,384]{1,0:T(8,128)}), f32[96,384]{1,0:T(8,128)}) %all-reduce.2.cloned.1.call-update) | async-done | bytes 147472 | tf_op jit(solution)/shard_map/psum | solution.py:27
  126.2 0.0 copy-done
  126.2 1.3 fusion.18
  127.5 1.9 %all_gather.7 = f32[96,384]{0,1:T(8,128)S(1)} all-gather(f32[96,192]{0,1:T(8,128)S(1)} %fusion.18), channel_id=1, replica_groups=mesh['wide'=16,'clus'=2] {'clus'}, dimensions={1}, use_global_device_ids=true | all-gather | bytes 221184 | tf_op jit(solution)/shard_map/all_gather | solution.py:29
  129.5 0.2 convolution_subtract_fusion
  129.7 0.1 fusion.12
  129.9 0.0 copy-done.1
  129.9 0.6 fusion.1
  130.5 2.6 %copy.23 = bf16[96,2,3840]{2,1,0:T(2,128)(2,1)} copy(bf16[96,2,3840]{2,0,1:T(8,128)(2,1)S(1)} %fusion.1) | data formatting | bytes 2949120 | tf_op jit(solution)/shard_map/convert_element_type | solution.py:39
  (5 shorter events, 0.1 us)
Async XLA Ops:
  6.5 119.7 %copy-start = (f32[384,192]{0,1:T(8,128)S(1)}, f32[384,192]{0,1:T(8,128)}, u32[]{:S(2)}) copy-start(f32[384,192]{0,1:T(8,128)} %param.13) | copy-start | bytes 884740
  6.5 9.2 %copy-start.2 = (s32[1,24]{1,0:T(1,128)S(1)}, s32[1,24]{1,0:T(1,128)}, u32[]{:S(2)}) copy-start(s32[1,24]{1,0:T(1,128)} %param.12) | copy-start | bytes 292
  6.5 119.7 %all-reduce.2.cloned.1.call-start = ((), (), s32[]{:S(2)}) async-start(), calls=%async_computation | async-start | bytes 294912 | tf_op jit(solution)/shard_map/psum | solution.py:27
  11.6 118.3 %copy-start.1 = (bf16[96,2,3840]{2,1,0:T(2,128)(2,1)S(1)}, bf16[96,2,3840]{2,1,0:T(2,128)(2,1)}, u32[]{:S(2)}) copy-start(bf16[96,2,3840]{2,1,0:T(2,128)(2,1)} %param.7) | copy-start | bytes 4423684
Sparse Core Ops, SparseCore 0:
  16.8 109.3 all-reduce.1
where the time goes:
time: 140 us
  waiting for transfers between devices  110 us (79%)
  between operations  14.2 us (10%)
  matrix products  5.34 us (4%)
  other arithmetic  4.31 us (3%)
  blocking collectives  3.92 us (3%)
  local copies, waits for them, and re-layouts  2.7 us (2%)
    psum x1, waiting for transfers between devices, per_device(): gsum = lax.psum(part_sum, 'wide')  110 us
  transfers between devices with their start and end apart: 1, of which 1 were waited for; matrix products, arithmetic and copies ran while one was open for 0% of the time, Pallas kernels for 0%

commit v1 on v0

--- a/solution.py
+++ b/solution.py
@@ -24,7 +24,9 @@
         rows_map[:, None] == lax.broadcasted_iota(jnp.int32, (cluster_rows, global_rows), 1)
     ).astype(jnp.float32)
     part_sum = jnp.dot(forward, one_hot, precision=hi)
-    gsum = lax.psum(part_sum, "wide")
+    gsum = part_sum
+    for hop in (1, 2, 4, 8):
+        gsum = gsum + lax.ppermute(gsum, "wide", [(dev, dev ^ hop) for dev in range(16)])
     beta_part = jnp.dot(gsum, coarse_inverse, precision=hi)
     beta = lax.all_gather(beta_part, "clus", axis=1, tiled=True)
     back = jnp.dot(beta, one_hot.T, precision=hi)

time: 140 us -> 41.3 us (0.29)
  waiting for transfers between devices: 110 us -> 16 us
  between operations: 14.2 us -> 0.8 us
  starting transfers between devices: 0.01 us -> 9.54 us
  matrix products: 5.34 us -> 3.67 us
    psum x1 -> x0, waiting for transfers between devices: 110 us -> none  [per_device(): gsum = lax.psum(part_sum, 'wide')]
    ppermute x0 -> x4, waiting for transfers between devices: none -> 16 us  [per_device(): lax.ppermute(gsum, 'wide', [(dev, dev ^ hop) for dev in range(16)])]
    ppermute x0 -> x4, starting transfers between devices: none -> 9.54 us  [per_device(): lax.ppermute(gsum, 'wide', [(dev, dev ^ hop) for dev in range(16)])]
  transfers between devices with their start and end apart: 1 -> 4, of which waited for: 1 -> 4; matrix products, arithmetic and copies ran while one was open for 0% -> 0% of each run, Pallas kernels for 0% -> 0%
where the time goes in v1:
time: 41.3 us; the launch traced here: 41.1 us
  waiting for transfers between devices  16 us (39%)
  starting transfers between devices  9.54 us (23%)
  other arithmetic  4.35 us (11%)
  blocking collectives  4.05 us (10%)
  matrix products  3.67 us (9%)
  local copies, waits for them, and re-layouts  2.69 us (7%)
  between operations  0.8 us (2%)
    ppermute x4, waiting for transfers between devices, per_device(): lax.ppermute(gsum, 'wide', [(dev, dev ^ hop) for dev in range(16)])  16 us
    ppermute x4, starting transfers between devices, per_device(): lax.ppermute(gsum, 'wide', [(dev, dev ^ hop) for dev in range(16)])  9.54 us
    convert_element_type x1, local copies, waits for them, and re-layouts, per_device(): return (duals.astype(jnp.float32) - delta).astype(jnp.bfloat16)  2.63 us
    another operation x2, other arithmetic, per_device(): lax.linalg.triangular_solve(lower, (forward - back).T, left_side=True, lo...  2.55 us
    all_gather x1, blocking collectives, per_device(): cluster_vec = lax.all_gather(local, 'clus', axis=1, tiled=True)  2.1 us
    all_gather x1, blocking collectives, per_device(): beta = lax.all_gather(beta_part, 'clus', axis=1, tiled=True)  1.95 us
    dot_general x1, matrix products, per_device(): jnp.einsum('rsi,ski->rsk', duals, masked, preferred_element_type=jnp.floa...  1.85 us
    select_n x1, other arithmetic, per_device(): masked = jnp.where(active[:, None, :], kernel, jnp.zeros_like(kernel))  0.98 us
  transfers between devices with their start and end apart: 4, of which 4 were waited for; matrix products, arithmetic and copies ran while one was open for 0% of the time, Pallas kernels for 0%

profile of v1, /device:TPU:0, one launch (start us, length us, event | category | flops | bytes accessed | tf_op | source)
XLA Modules:
  0.0 41.1 jit_solution(3064429446144641165)
XLA Ops:
  0.0 0.0 copy-start
  0.0 0.0 copy-start.2
  0.7 0.7 %fusion.18 = f32[1,24,24]{2,1,0:T(8,128)S(1)} fusion(f32[1,24,24]{2,1,0:T(8,128)} %param.11), kind=kLoop, calls=%fused_computation.22 | loop fusion | flops 1152 | bytes 4608 | tf_op jit(solution)/shard_map/triangular_solve | solution.py:33
  1.4 1.8 %custom-call.5 = f32[1,24,24]{1,2,0:T(8,128)S(1)} custom-call(f32[1,24,24]{2,1,0:T(8,128)S(1)} %fusion.18), custom_call_target="InvertDiagBlocksLowerTriangular" | custom-call | tf_op jit(solution)/shard_map/triangular_solve | solution.py:33
  3.3 0.8 %compare_and_fusion = pred[2,3840]{1,0:T(4,128)(4,1)S(1)} fusion(pred[2]{0:T(512)(128)(4,1)S(1)} %iota_compare_fusion.4, s32[2]{0:T(128)} %param.10), kind=kLoop, calls=%fused_computation.12 | loop fusion | flops 15360 | bytes 7690 | tf_op jit(solution)/shard_map/and | solution.py:13
  4.0 1.0 %broadcast_select_fusion = bf16[2,6,3840]{2,0,1:T(2,128)(2,1)S(1)} fusion(bf16[2,6,3840]{2,0,1:T(2,128)(2,1)} %param.8, pred[2,3840]{1,0:T(4,128)(4,1)S(1)} %compare_and_fusion), kind=kLoop, calls=%fused_computation.7 | loop fusion | flops 46080 | bytes 192000 | tf_op jit(solution)/shard_map/jit(_where)/select_n | solution.py:14
  5.0 1.9 %fusion.4 = f32[96,2,6]{0,2,1:T(8,128)S(1)} fusion(bf16[96,2,3840]{2,1,0:T(2,128)(2,1)} %param.7, bf16[2,6,3840]{2,0,1:T(2,128)(2,1)S(1)} %broadcast_select_fusion), kind=kOutput, calls=%fused_computation.6 | convolution fusion | flops 8847360 | bytes 1571328 | tf_op jit(solution)/shard_map/rsi,ski->rsk/dot_general | solution.py:15
  6.9 0.0 copy-start.1
  6.9 2.1 %all-gather = f32[2,12,96]{2,1,0:T(8,128)S(1)} all-gather(f32[1,12,96]{2,1,0:T(8,128)S(1)} %bitcast.33), channel_id=1, replica_groups=mesh['wide'=16,'clus'=2] {'clus'}, dimensions={0}, use_global_device_ids=true | all-gather | bytes 13824 | tf_op jit(solution)/shard_map/all_gather | solution.py:17
  9.0 0.2 fusion.16
  9.2 0.0 copy-done.2
  9.2 0.3 fusion.11
  9.5 2.9 %collective-permute-start = (f32[96,384]{1,0:T(8,128)S(1)}, f32[96,384]{1,0:T(8,128)S(1)}, u32[]{:S(2)}, u32[]{:S(2)}) collective-permute-start(f32[96,384]{1,0:T(8,128)S(1)} %fusion.11), channel_id=1, source_target_pairs={{0,2},{2,0},{4,6},{6,4},{8,10},{10,8},{12,14},{14,12},{16,18},{18,... | collective-permute-start | bytes 442376 | tf_op jit(solution)/shard_map/ppermute | solution.py:29
  12.4 4.2 %collective-permute-done = f32[96,384]{1,0:T(8,128)S(1)} collective-permute-done((f32[96,384]{1,0:T(8,128)S(1)}, f32[96,384]{1,0:T(8,128)S(1)}, u32[]{:S(2)}, u32[]{:S(2)}) %collective-permute-start) | collective-permute-done | bytes 147488 | tf_op jit(solution)/shard_map/ppermute | solution.py:29
  16.6 1.8 %collective-permute-start.1 = (f32[96,384]{1,0:T(8,128)S(1)}, f32[96,384]{1,0:T(8,128)S(1)}, u32[]{:S(2)}, u32[]{:S(2)}) collective-permute-start(f32[96,384]{1,0:T(8,128)S(1)} %add.19), channel_id=1, source_target_pairs={{0,4},{2,6},{4,0},{6,2},{8,12},{10,14},{12,8},{14,10},{16,20},{18,... | collective-permute-start | bytes 442376 | tf_op jit(solution)/shard_map/ppermute | solution.py:29
  18.4 3.6 %collective-permute-done.1 = f32[96,384]{1,0:T(8,128)S(1)} collective-permute-done((f32[96,384]{1,0:T(8,128)S(1)}, f32[96,384]{1,0:T(8,128)S(1)}, u32[]{:S(2)}, u32[]{:S(2)}) %collective-permute-start.1) | collective-permute-done | bytes 147488 | tf_op jit(solution)/shard_map/ppermute | solution.py:29
  22.0 1.7 %collective-permute-start.2 = (f32[96,384]{1,0:T(8,128)S(1)}, f32[96,384]{1,0:T(8,128)S(1)}, u32[]{:S(2)}, u32[]{:S(2)}) collective-permute-start(f32[96,384]{1,0:T(8,128)S(1)} %add.20), channel_id=1, source_target_pairs={{0,8},{2,10},{4,12},{6,14},{8,0},{10,2},{12,4},{14,6},{16,24},{18,... | collective-permute-start | bytes 442376 | tf_op jit(solution)/shard_map/ppermute | solution.py:29
  23.7 3.5 %collective-permute-done.2 = f32[96,384]{1,0:T(8,128)S(1)} collective-permute-done((f32[96,384]{1,0:T(8,128)S(1)}, f32[96,384]{1,0:T(8,128)S(1)}, u32[]{:S(2)}, u32[]{:S(2)}) %collective-permute-start.2) | collective-permute-done | bytes 147488 | tf_op jit(solution)/shard_map/ppermute | solution.py:29
  27.2 3.1 %collective-permute-start.3 = (f32[96,384]{1,0:T(8,128)S(1)}, f32[96,384]{1,0:T(8,128)S(1)}, u32[]{:S(2)}, u32[]{:S(2)}) collective-permute-start(f32[96,384]{1,0:T(8,128)S(1)} %add.21), channel_id=1, source_target_pairs={{0,16},{2,18},{4,20},{6,22},{8,24},{10,26},{12,28},{14,30},{16,0},... | collective-permute-start | bytes 442376 | tf_op jit(solution)/shard_map/ppermute | solution.py:29
  30.4 4.7 %collective-permute-done.3 = f32[96,384]{1,0:T(8,128)S(1)} collective-permute-done((f32[96,384]{1,0:T(8,128)S(1)}, f32[96,384]{1,0:T(8,128)S(1)}, u32[]{:S(2)}, u32[]{:S(2)}) %collective-permute-start.3) | collective-permute-done | bytes 147488 | tf_op jit(solution)/shard_map/ppermute | solution.py:29
  35.1 0.0 copy-done
  35.1 0.4 %fusion.7 = f32[96,192]{0,1:T(8,128)S(1)} fusion(f32[384,192]{0,1:T(8,128)S(1)} %copy-done, f32[96,384]{1,0:T(8,128)S(1)} %add.21, f32[96,384]{1,0:T(8,128)S(1)} %collective-permute-done.3), kind=kOutput, calls=%fused_computation.8 | convolution fusion | flops 84971520 | bytes 663552 | tf_op jit(solution)/shard_map/dot_general | solution.py:30
  35.5 1.9 %all_gather.7 = f32[96,384]{0,1:T(8,128)S(1)} all-gather(f32[96,192]{0,1:T(8,128)S(1)} %fusion.7), channel_id=1, replica_groups=mesh['wide'=16,'clus'=2] {'clus'}, dimensions={1}, use_global_device_ids=true | all-gather | bytes 221184 | tf_op jit(solution)/shard_map/all_gather | solution.py:31
  37.4 0.2 convolution_subtract_fusion
  37.7 0.1 fusion.14
  37.8 0.0 copy-done.1
  37.9 0.6 %fusion.1 = bf16[96,2,3840]{2,0,1:T(8,128)(2,1)S(1)} fusion(bf16[96,2,6]{0,2,1:T(8,128)(2,1)S(1)} %convert_element_type.19, bf16[96,2,3840]{2,1,0:T(2,128)(2,1)S(1)} %copy-done.1, bf16[2,6,3840]{2,0,1:T(2,128)(2,1)S(1)} %broadcast_select_fusion), kind=kOutput, calls=%fused_computation.2 | convolution fusion | flops 11059200 | bytes 3043584 | tf_op jit(solution)/shard_map/rsk,ski->rsi/dot_general | solution.py:40
  38.4 2.6 %copy.23 = bf16[96,2,3840]{2,1,0:T(2,128)(2,1)} copy(bf16[96,2,3840]{2,0,1:T(8,128)(2,1)S(1)} %fusion.1) | data formatting | bytes 2949120 | tf_op jit(solution)/shard_map/convert_element_type | solution.py:41
  (8 shorter events, 0.1 us)
Async XLA Ops:
  0.0 35.1 %copy-start = (f32[384,192]{0,1:T(8,128)S(1)}, f32[384,192]{0,1:T(8,128)}, u32[]{:S(2)}) copy-start(f32[384,192]{0,1:T(8,128)} %param.13) | copy-start | bytes 884740
  0.0 9.2 %copy-start.2 = (s32[1,24]{1,0:T(1,128)S(1)}, s32[1,24]{1,0:T(1,128)}, u32[]{:S(2)}) copy-start(s32[1,24]{1,0:T(1,128)} %param.12) | copy-start | bytes 292
  6.9 31.0 %copy-start.1 = (bf16[96,2,3840]{2,1,0:T(2,128)(2,1)S(1)}, bf16[96,2,3840]{2,1,0:T(2,128)(2,1)}, u32[]{:S(2)}) copy-start(bf16[96,2,3840]{2,1,0:T(2,128)(2,1)} %param.7) | copy-start | bytes 4423684
  9.5 7.1 %collective-permute-start = (f32[96,384]{1,0:T(8,128)S(1)}, f32[96,384]{1,0:T(8,128)S(1)}, u32[]{:S(2)}, u32[]{:S(2)}) collective-permute-start(f32[96,384]{1,0:T(8,128)S(1)} %fusion.11), channel_id=1, source_target_pairs={{0,2},{2,0},{4,6},{6,4},{8,10},{10,8},{12,14},{14,12},{16,18},{18,... | collective-permute-start | bytes 442376 | tf_op jit(solution)/shard_map/ppermute | solution.py:29
  16.6 5.4 %collective-permute-start.1 = (f32[96,384]{1,0:T(8,128)S(1)}, f32[96,384]{1,0:T(8,128)S(1)}, u32[]{:S(2)}, u32[]{:S(2)}) collective-permute-start(f32[96,384]{1,0:T(8,128)S(1)} %add.19), channel_id=1, source_target_pairs={{0,4},{2,6},{4,0},{6,2},{8,12},{10,14},{12,8},{14,10},{16,20},{18,... | collective-permute-start | bytes 442376 | tf_op jit(solution)/shard_map/ppermute | solution.py:29
  22.0 5.2 %collective-permute-start.2 = (f32[96,384]{1,0:T(8,128)S(1)}, f32[96,384]{1,0:T(8,128)S(1)}, u32[]{:S(2)}, u32[]{:S(2)}) collective-permute-start(f32[96,384]{1,0:T(8,128)S(1)} %add.20), channel_id=1, source_target_pairs={{0,8},{2,10},{4,12},{6,14},{8,0},{10,2},{12,4},{14,6},{16,24},{18,... | collective-permute-start | bytes 442376 | tf_op jit(solution)/shard_map/ppermute | solution.py:29
  27.2 7.8 %collective-permute-start.3 = (f32[96,384]{1,0:T(8,128)S(1)}, f32[96,384]{1,0:T(8,128)S(1)}, u32[]{:S(2)}, u32[]{:S(2)}) collective-permute-start(f32[96,384]{1,0:T(8,128)S(1)} %add.21), channel_id=1, source_target_pairs={{0,16},{2,18},{4,20},{6,22},{8,24},{10,26},{12,28},{14,30},{16,0},... | collective-permute-start | bytes 442376 | tf_op jit(solution)/shard_map/ppermute | solution.py:29
